TPU v7x, 128 devices: a whole 4x4x4 slice. The times are simulated.
128 devices in a mesh: grp: 8 (over y, core), aux: 16 (over x, z).
Axes of the slice: x: 4, y: 4, z: 4, core: 2. Of those that a mesh axis runs over, the one named last changes fastest.
Arguments:
- integral_tiles: bfloat16 [8, 16, 12, 32, 128, 128], P('grp', 'aux'), may hold values from -6 to 6
- row_blocks: int32 [8, 16, 12], P('grp', 'aux'), may hold values from 0 to 31
- col_blocks: int32 [8, 16, 12], P('grp', 'aux'), may hold values from 0 to 3
- aux_blocks: int32 [8, 16, 12], P('grp', 'aux'), may hold values from 0 to 15
- tile_counts: int32 [8, 16], P('grp', 'aux'), may hold values from 1 to 12, as said below
- occ_coeffs: bfloat16 [8, 4096], P(None, 'grp'), may hold values from -0.5 to 0.5
- vir_coeffs: bfloat16 [4096, 1024], P('grp'), may hold values from -0.5 to 0.5
Outputs:
- pair_factors: float32 [8192, 8192], P(('grp', 'aux'))
Inputs may be any that keep to these rules, and one draw needn't show every extreme that they name: `tile_counts`: tile counts of the devices; some device holds exactly 12 kept tiles.
All inputs are finite; a program needn't handle non-finite values.
Results may differ from a plain program's by a relative error of at most 0.0029.
Values may be sent and summed in bfloat16 or wider, within the bound.
A program may use at most 128 MiB of HBM per device.

v0:
```python
import jax
import jax.numpy as jnp
from jax import lax
from jax.sharding import PartitionSpec as P

O = 8
V = 1024
BLK = 128
PB = 32
PDEV = 512
KMAX = 12


def tile_term(tile, row_block, col_block, occ_whole, vir_coeffs):
    occ_block = lax.dynamic_slice_in_dim(occ_whole, row_block * BLK, BLK, 1)
    half_tile = jnp.einsum(
        "im,pmn->ipn", occ_block, tile, preferred_element_type=jnp.float32
    ).astype(jnp.bfloat16)
    vir_block = lax.dynamic_slice_in_dim(vir_coeffs, col_block * BLK, BLK, 0)
    term = jnp.einsum("na,ipn->iap", vir_block, half_tile, preferred_element_type=jnp.float32)
    return term.reshape(O * V, PB)


def shards(integral_tiles, row_blocks, col_blocks, aux_blocks, tile_counts, occ_coeffs, vir_coeffs):
    occ_whole = lax.all_gather(occ_coeffs, "grp", axis=1, tiled=True)
    my_tiles = integral_tiles[0, 0]
    my_rows = row_blocks[0, 0]
    my_cols = col_blocks[0, 0]
    my_aux = aux_blocks[0, 0]
    my_count = tile_counts[0, 0]
    group_size = lax.axis_size("grp")
    aux_size = lax.axis_size("aux")
    partial_value = jnp.zeros((O * V, PDEV), jnp.float32)

    def add_tile(slot, partial_value, weight):
        term = tile_term(my_tiles[slot], my_rows[slot], my_cols[slot], occ_whole, vir_coeffs)
        start = my_aux[slot] * PB
        current = lax.dynamic_slice_in_dim(partial_value, start, PB, 1)
        return lax.dynamic_update_slice_in_dim(partial_value, current + weight * term, start, 1)

    def padded_step(slot, partial_value):
        weight = (slot < my_count).astype(jnp.float32)
        return add_tile(slot, partial_value, weight)

    partial_value = lax.fori_loop(0, KMAX, padded_step, partial_value)
    share = O * V // (group_size * aux_size)
    reordered = (
        partial_value.reshape(group_size, aux_size, share, PDEV)
        .transpose(1, 0, 2, 3)
        .reshape(O * V, PDEV)
    )
    regrouped = lax.all_to_all(reordered, "aux", split_axis=0, concat_axis=1, tiled=True)
    pair_factors = lax.psum_scatter(regrouped, "grp", scatter_dimension=0, tiled=True)
    return pair_factors


def solution(mesh):
    in_specs = (
        P("grp", "aux", None, None, None, None),
        P("grp", "aux", None),
        P("grp", "aux", None),
        P("grp", "aux", None),
        P("grp", "aux"),
        P(None, "grp"),
        P("grp", None),
    )
    out_specs = P(("grp", "aux"), None)
    return jax.shard_map(shards, mesh=mesh, in_specs=in_specs, out_specs=out_specs, check_vma=False)
```

profile of v0, /device:TPU:0, one launch (start us, length us, event | category | flops | bytes accessed | tf_op | source)
XLA Modules:
  0.0 491.2 jit_solution(9957678706698154882)
XLA Ops:
  6.5 13.7 %all_gather.3 = bf16[8,4096]{1,0:T(8,128)(2,1)S(1)} all-gather(bf16[8,512]{1,0:T(8,128)(2,1)} %param.14), channel_id=1, replica_groups=mesh['grp'=8,'aux'=16] {'grp'}, dimensions={1}, use_global_device_ids=true | all-gather | bytes 73728 | tf_op jit(solution)/shard_map/all_gather | solution.py:25
  20.2 7.8 %broadcast_in_dim.3 = f32[8192,512]{0,1:T(8,128)} broadcast(f32[]{:T(128)} %constant.52.clone.1), dimensions={} | broadcast | bytes 16777220 | tf_op jit(solution)/shard_map/broadcast_in_dim | solution.py:33
  28.0 113.7 %while.13 = (s32[]{:T(128)}, f32[8192,512]{0,1:T(8,128)}, s32[12]{0:T(128)S(1)}, s32[]{:T(128)}, s32[12]{0:T(128)S(1)}, /*index=5*/bf16[8,4096]{1,0:T(8,128)(2,1...) while((s32[]{:T(128)}, f32[8192,512]{0,1:T(8,128)}, ...), condition=%wide.region_1.0_spmd, body=%wide.region_0.0_spmd.sunk | while | flops 76054544 | bytes 7735653 | solution.py:45
  32.4 1.5 convolution_convert_fusion.2
  35.2 2.3 add_dynamic-update-slice_fusion.2
  41.9 1.5 convolution_convert_fusion.2
  44.7 2.3 add_dynamic-update-slice_fusion.2
  51.3 1.5 convolution_convert_fusion.2
  54.1 2.3 add_dynamic-update-slice_fusion.2
  60.8 1.5 convolution_convert_fusion.2
  63.6 2.3 add_dynamic-update-slice_fusion.2
  70.3 1.5 convolution_convert_fusion.2
  73.1 2.3 add_dynamic-update-slice_fusion.2
  79.8 1.5 convolution_convert_fusion.2
  82.6 2.3 add_dynamic-update-slice_fusion.2
  89.2 1.5 convolution_convert_fusion.2
  92.0 2.3 add_dynamic-update-slice_fusion.2
  98.7 1.5 convolution_convert_fusion.2
  101.5 2.3 add_dynamic-update-slice_fusion.2
  108.2 1.5 convolution_convert_fusion.2
  111.0 2.3 add_dynamic-update-slice_fusion.2
  117.7 1.5 convolution_convert_fusion.2
  120.5 2.3 add_dynamic-update-slice_fusion.2
  127.1 1.5 convolution_convert_fusion.2
  129.9 2.3 add_dynamic-update-slice_fusion.2
  139.4 2.3 add_dynamic-update-slice_fusion.2
  141.7 17.5 %copy.26 = f32[8192,512]{1,0:T(8,128)} copy(f32[8192,512]{0,1:T(8,128)} %get-tuple-element.159) | data formatting | bytes 33554432 | tf_op jit(solution)/shard_map/while | solution.py:45
  159.2 7.1 %copy.27 = f32[16,8,64,512]{3,2,1,0:T(8,128)S(1)} copy(f32[16,8,64,512]{3,2,0,1:T(8,128)} %bitcast.45) | data formatting | bytes 33554432 | tf_op jit(solution)/shard_map/transpose | solution.py:49
  166.3 193.9 %all_to_all.19 = f32[16,512,512]{2,1,0:T(8,128)} all-to-all(f32[16,512,512]{2,1,0:T(8,128)S(1)} %bitcast.46), channel_id=1, replica_groups=mesh['grp'=8,'aux'=16] {'aux'}, dimensions={0} | all-to-all | bytes 33554432 | tf_op jit(solution)/shard_map/all_to_all | solution.py:52
  360.2 17.6 %copy.28 = f32[512,16,512]{0,2,1:T(8,128)} copy(f32[512,16,512]{2,0,1:T(8,128)} %bitcast.47) | data formatting | bytes 33554432 | tf_op jit(solution)/shard_map/all_to_all | solution.py:52
  377.8 17.4 %copy.30 = f32[512,8192]{1,0:T(8,128)} copy(f32[512,8192]{0,1:T(8,128)} %bitcast.48) | data formatting | bytes 33554432
  395.2 89.2 %reduce-scatter.4.cloned.1.call-done = f32[64,8192]{1,0:T(8,128)} async-done(((f32[512,8192]{1,0:T(8,128)}), f32[64,8192]{1,0:T(8,128)}) %reduce-scatter.4.cloned.1.call-update) | async-done | bytes 2097168 | tf_op jit(solution)/shard_map/reduce_scatter | solution.py:53
  (69 shorter events, 39.5 us)
Async XLA Ops:
  6.5 21.5 %copy-start = (s32[1,1,12]{2,1,0:T(1,128)S(1)}, s32[1,1,12]{2,1,0:T(1,128)}, u32[]{:S(2)}) copy-start(s32[1,1,12]{2,1,0:T(1,128)} %param.12) | copy-start | bytes 148
  6.5 21.5 %copy-start.2 = (s32[1,1,12]{2,1,0:T(1,128)S(1)}, s32[1,1,12]{2,1,0:T(1,128)}, u32[]{:S(2)}) copy-start(s32[1,1,12]{2,1,0:T(1,128)} %param.11) | copy-start | bytes 148
  6.5 21.5 %copy-start.1 = (s32[1,1,12]{2,1,0:T(1,128)S(1)}, s32[1,1,12]{2,1,0:T(1,128)}, u32[]{:S(2)}) copy-start(s32[1,1,12]{2,1,0:T(1,128)} %param.10) | copy-start | bytes 148
  6.5 477.9 %reduce-scatter.4.cloned.1.call-start = ((), (), s32[]{:S(2)}) async-start(), calls=%async_computation.2 | async-start | bytes 18874368 | tf_op jit(solution)/shard_map/reduce_scatter | solution.py:53
Sparse Core Ops, SparseCore 0:
  395.3 89.0 reduce-scatter.3
where the time goes:
time: 494 us; the launch traced here: 491 us
  blocking collectives  208 us (42%)
  local copies, waits for them, and re-layouts  90.4 us (18%)
  waiting for transfers between devices  89.2 us (18%)
  matrix products  32.6 us (7%)
  loops' own time  30.3 us (6%)
  other arithmetic  27.9 us (6%)
  between operations  13.4 us (3%)
    all_to_all x1, blocking collectives, shards(): lax.all_to_all(reordered, 'aux', split_axis=0, concat_axis=1, tiled=True)  194 us
    reduce_scatter x1, waiting for transfers between devices, shards(): lax.psum_scatter(regrouped, 'grp', scatter_dimension=0, tiled=True)  89.2 us
    another operation x1, loops' own time, shards(): partial_value = lax.fori_loop(0, KMAX, padded_step, partial_value)  30.3 us
    dynamic_update_slice x12, other arithmetic, add_tile(): lax.dynamic_update_slice_in_dim(partial_value, current + weight * term, s...  27.9 us
    dot_general x12, matrix products, tile_term(): jnp.einsum('im,pmn->ipn', occ_block, tile, preferred_element_type=jnp.flo...  17.6 us
    all_to_all x1, local copies, waits for them, and re-layouts, shards(): lax.all_to_all(reordered, 'aux', split_axis=0, concat_axis=1, tiled=True)  17.6 us
    while x1, local copies, waits for them, and re-layouts, shards(): partial_value = lax.fori_loop(0, KMAX, padded_step, partial_value)  17.5 us
    unnamed x7, local copies, waits for them, and re-layouts  17.4 us
  transfers between devices with their start and end apart: 1, of which 1 were waited for; matrix products, arithmetic and copies ran while one was open for 0% of the time, Pallas kernels for 0%

commit v1 on v0

v1 whole, which is shorter than its diff:
```python
import functools

import jax
import jax.numpy as jnp
from jax import lax
from jax.experimental import pallas as pl
from jax.experimental.pallas import tpu as pltpu
from jax.sharding import PartitionSpec as P

O = 8
V = 1024
BLK = 128
PB = 32
PDEV = 512
KMAX = 12
G = 8
NZ = 4
CH = 4
CT = KMAX // CH
MESH = pl.DeviceIdType.MESH


def rcopy(src, dst, ssem, rsem, dev):
    return pltpu.make_async_remote_copy(
        src_ref=src, dst_ref=dst, send_sem=ssem, recv_sem=rsem, device_id=dev, device_id_type=MESH
    )


def where_am_i():
    g = lax.axis_index("grp")
    a = lax.axis_index("aux")
    return g, a, lax.div(g, 2), lax.rem(g, 2), lax.div(a, NZ), lax.rem(a, NZ)


def spread_kernel(
    rows_ref, tiles_ref, cols_ref, aux_ref, count_ref, occ_ref, vir_ref,
    h_ref, v_ref, m_ref,
    tile_v, occ_all, meta_own, stage, hbuf,
    tile_sem, own_sem,
    occ_ss, occ_rs, meta_ss, meta_rs, mx_sem,
    h_ss, h_rs, hx_ss, hx_rs,
    vy_ss, vy_rs, vz_ss, vz_rs, vo_ss, vo_rs, vs_ss, vs_rs,
):
    g, a, y, c, x, z = where_am_i()
    s = lax.rem(x, 2)
    mate = (g, (x + 1 - 2 * s) * NZ + z)
    twin = (2 * y + 1 - c, a)
    xb = (x, 3 - x)

    def tile_copy(k):
        return pltpu.make_async_copy(tiles_ref.at[k], tile_v.at[k], tile_sem.at[k])

    for k in range(KMAX):
        tile_copy(k).start()

    def vir_cols(j):
        return vir_ref.at[:, :, pl.ds(pl.multiple_of(xb[j] * 256, 256), 256)]

    v_own = [pltpu.make_async_copy(vir_cols(j), v_ref.at[g, :, j], own_sem.at[j]) for j in range(2)]
    for cp in v_own:
        cp.start()

    for b in range(4):
        occ_all[g, b] = occ_ref[:, b * BLK:(b + 1) * BLK]
    meta_own[...] = jnp.zeros_like(meta_own)
    meta_own[0:1, 0:KMAX] = cols_ref[...]
    meta_own[1:2, 0:KMAX] = aux_ref[...]
    meta_own[2:3, 0:1] = count_ref[...]
    m_own = pltpu.make_async_copy(meta_own, m_ref.at[s, g], own_sem.at[2])
    m_own.start()

    peers = [lax.rem(g + d, G) for d in range(1, G)]
    ypeers = [2 * lax.rem(y + d, 4) + c for d in range(1, 4)]
    zpeers = [lax.rem(z + d, NZ) for d in range(1, NZ)]

    barrier = pltpu.get_barrier_semaphore()
    for p in peers:
        pl.semaphore_signal(barrier, inc=1, device_id=(p, a), device_id_type=MESH)
    pl.semaphore_signal(barrier, inc=1, device_id=mate, device_id_type=MESH)
    for zp in zpeers:
        pl.semaphore_signal(barrier, inc=1, device_id=(g, x * NZ + zp), device_id_type=MESH)
    pl.semaphore_wait(barrier, 11)

    def occ_copy(src, d, dev):
        return rcopy(occ_all.at[src], occ_all.at[src], occ_ss.at[d], occ_rs.at[src], dev)

    def meta_copy(src, d, dev):
        return rcopy(meta_own, m_ref.at[s, src], meta_ss.at[d], meta_rs.at[src], dev)

    for d, p in enumerate(peers):
        occ_copy(g, d, (p, a)).start()

    def vy_copy(src, d, j, dev):
        return rcopy(
            vir_ref.at[z, :, pl.ds(pl.multiple_of(xb[j] * 256, 256), 256)],
            v_ref.at[src, z, j], vy_ss.at[d, j], vy_rs.at[lax.div(src, 2), j], dev,
        )

    for d, p in enumerate(ypeers):
        for j in range(2):
            vy_copy(g, d, j, (p, a)).start()
    for d, p in enumerate(peers):
        meta_copy(g, d, (p, a)).start()

    def vo_copy(src, j):
        return rcopy(vir_cols(j), v_ref.at[src, :, j], vo_ss.at[j], vo_rs.at[j], twin)

    for j in range(2):
        vo_copy(g, j).start()

    for d, p in enumerate(peers):
        occ_copy(p, d, (p, a)).wait_recv()

    def compute(chunk):
        def one(t, carry):
            k = chunk * CT + t
            tile_copy(k).wait()
            row = rows_ref[k]
            occ = occ_all[lax.div(row, 4), lax.rem(row, 4)]
            for pp in range(PB // 2):
                rhs = jnp.concatenate([tile_v[k, 2 * pp], tile_v[k, 2 * pp + 1]], axis=1)
                out = jnp.dot(occ, rhs, preferred_element_type=jnp.float32)
                stage[16 * pp:16 * pp + 8, :] = out[:, :BLK]
                stage[16 * pp + 8:16 * pp + 16, :] = out[:, BLK:]
            for i in range(O):
                hbuf[i, chunk, t] = stage[pl.ds(i, PB, stride=O), :].astype(jnp.bfloat16)
            return carry

        lax.fori_loop(0, CT, one, 0)

    def h_copy(dst_g, src, chunk, d, dev):
        return rcopy(
            hbuf.at[dst_g, chunk], h_ref.at[s, chunk, src], h_ss.at[chunk, d], h_rs.at[chunk, src], dev
        )

    def h_own(chunk):
        return pltpu.make_async_copy(hbuf.at[g, chunk], h_ref.at[s, chunk, g], own_sem.at[3 + chunk])

    def hx_copy(side, chunk):
        return rcopy(h_ref.at[side, chunk], h_ref.at[side, chunk], hx_ss.at[chunk], hx_rs.at[chunk], mate)

    def mx_copy(side):
        return rcopy(m_ref.at[side], m_ref.at[side], mx_sem.at[0], mx_sem.at[1], mate)

    def forward_h(chunk):
        h_own(chunk).wait()
        for d, p in enumerate(peers):
            h_copy(p, p, chunk, d, (p, a)).wait_recv()
        hx_copy(s, chunk).start()

    def vz_copy(src, src_z, d, e, dev):
        return rcopy(
            v_ref.at[src, src_z], v_ref.at[src, src_z], vz_ss.at[d, e],
            vz_rs.at[lax.div(src, 2), src_z], dev,
        )

    def vs_copy(src, d):
        return rcopy(v_ref.at[src], v_ref.at[src], vs_ss.at[d], vs_rs.at[lax.div(src, 2)], twin)

    for chunk in range(CH):
        compute(chunk)
        for d, p in enumerate(peers):
            h_copy(p, g, chunk, d, (p, a)).start()
        h_own(chunk).start()
        if chunk == 0:
            for d, p in enumerate(ypeers):
                for j in range(2):
                    vy_copy(p, d, j, (p, a)).wait_recv()
                for e, zp in enumerate(zpeers):
                    vz_copy(p, z, d, e, (g, x * NZ + zp)).start()
        if chunk == 1:
            m_own.wait()
            for d, p in enumerate(peers):
                meta_copy(p, d, (p, a)).wait_recv()
            mx_copy(s).start()
        if chunk >= 1:
            forward_h(chunk - 1)
    forward_h(CH - 1)
    for d, p in enumerate(ypeers):
        for e, zp in enumerate(zpeers):
            vz_copy(p, zp, d, e, (g, x * NZ + zp)).wait_recv()
        vs_copy(p, d).start()

    for j in range(2):
        vo_copy(2 * y + 1 - c, j).wait_recv()
        v_own[j].wait()
    mx_copy(1 - s).wait_recv()
    for chunk in range(CH):
        hx_copy(1 - s, chunk).wait_recv()
    for d in range(1, 4):
        vs_copy(2 * lax.rem(y + d, 4) + 1 - c, d - 1).wait_recv()

    for d, p in enumerate(peers):
        occ_copy(g, d, (p, a)).wait_send()
        meta_copy(g, d, (p, a)).wait_send()
        for chunk in range(CH):
            h_copy(p, g, chunk, d, (p, a)).wait_send()
    for d, p in enumerate(ypeers):
        for j in range(2):
            vy_copy(g, d, j, (p, a)).wait_send()
        for e, zp in enumerate(zpeers):
            vz_copy(p, z, d, e, (g, x * NZ + zp)).wait_send()
        vs_copy(p, d).wait_send()
    for j in range(2):
        vo_copy(g, j).wait_send()
    mx_copy(s).wait_send()
    for chunk in range(CH):
        hx_copy(s, chunk).wait_send()


def spread(rows, tiles, cols, aux, count, occ, vir):
    any_spec = pl.BlockSpec(memory_space=pl.ANY)
    vmem = pl.BlockSpec(memory_space=pltpu.VMEM)
    dma = pltpu.SemaphoreType.DMA
    return pl.pallas_call(
        spread_kernel,
        out_shape=(
            jax.ShapeDtypeStruct((2, CH, G, CT, PB, BLK), jnp.bfloat16),
            jax.ShapeDtypeStruct((G, 4, 2, BLK, 256), jnp.bfloat16),
            jax.ShapeDtypeStruct((2, G, 8, 128), jnp.int32),
        ),
        in_specs=[pl.BlockSpec(memory_space=pltpu.SMEM), any_spec, vmem, vmem, vmem, vmem, any_spec],
        out_specs=(any_spec, any_spec, any_spec),
        scratch_shapes=[
            pltpu.VMEM((KMAX, PB, BLK, BLK), jnp.bfloat16),
            pltpu.VMEM((G, 4, O, BLK), jnp.bfloat16),
            pltpu.VMEM((8, 128), jnp.int32),
            pltpu.VMEM((PB * O, BLK), jnp.float32),
            pltpu.VMEM((O, CH, CT, PB, BLK), jnp.bfloat16),
            dma((KMAX,)), dma((3 + CH,)),
            dma((7,)), dma((G,)), dma((7,)), dma((G,)), dma((2,)),
            dma((CH, 7)), dma((CH, G)), dma((CH,)), dma((CH,)),
            dma((3, 2)), dma((4, 2)), dma((3, 3)), dma((4, NZ)),
            dma((2,)), dma((2,)), dma((3,)), dma((4,)),
        ],
        compiler_params=pltpu.CompilerParams(
            collective_id=0, has_side_effects=True, vmem_limit_bytes=40 * 1024 * 1024
        ),
        name="spread",
    )(rows, tiles, cols, aux, count, occ, vir)


UN = 6


def contract_kernel(m_ref, h_ref, v_ref, out_ref, acc):
    s = pl.program_id(0)
    acc[...] = jnp.zeros_like(acc)

    def group(g, carry):
        count = m_ref[s, g, 2, 0]
        for part in range(KMAX // UN):
            @pl.when(count > part * UN)
            def _():
                for t in range(UN):
                    k = part * UN + t
                    col = m_ref[s, g, 0, k]
                    start = pl.multiple_of(m_ref[s, g, 1, k] * PB, PB)
                    half = h_ref[0, k // CT, g, k % CT]
                    half = jnp.where(k < count, half, jnp.zeros_like(half))
                    for j in range(2):
                        term = jnp.dot(half, v_ref[g, col, j], preferred_element_type=jnp.float32)
                        acc[j, pl.ds(start, PB), :] += term
        return carry

    lax.fori_loop(0, G, group, 0)
    for j in range(2):
        out_ref[0, j * 256:(j + 1) * 256, :] = acc[j].T.astype(jnp.bfloat16)


def contract(meta, halves, vir):
    return pl.pallas_call(
        contract_kernel,
        out_shape=jax.ShapeDtypeStruct((2, 512, PDEV), jnp.bfloat16),
        grid_spec=pltpu.PrefetchScalarGridSpec(
            num_scalar_prefetch=1,
            grid=(2,),
            in_specs=[
                pl.BlockSpec((1, CH, G, CT, PB, BLK), lambda s, m: (s, 0, 0, 0, 0, 0)),
                pl.BlockSpec((G, 4, 2, BLK, 256), lambda s, m: (0, 0, 0, 0, 0)),
            ],
            out_specs=pl.BlockSpec((1, 512, PDEV), lambda s, m: (s, 0, 0)),
            scratch_shapes=[pltpu.VMEM((2, PDEV, 256), jnp.float32)],
        ),
        compiler_params=pltpu.CompilerParams(vmem_limit_bytes=40 * 1024 * 1024),
        name="contract",
    )(meta, halves, vir)


def deliver_kernel(r_ref, o_ref, own_sem, ss, rs):
    g, a, y, c, x, z = where_am_i()
    s = lax.rem(x, 2)
    xb = (x, 3 - x)
    dests = [(j, lax.rem(z + d, NZ), d) for d in range(NZ) for j in range(2) if (d, j) != (0, 0)]

    barrier = pltpu.get_barrier_semaphore()
    for j, zp, d in dests:
        pl.semaphore_signal(barrier, inc=1, device_id=(g, xb[j] * NZ + zp), device_id_type=MESH)

    def columns(x_src, z_src, side):
        first = ((x_src - lax.rem(x_src, 2) + side) * NZ + z_src) * PDEV
        return o_ref.at[:, pl.ds(pl.multiple_of(first, PDEV), PDEV)]

    def piece(j, zp, side):
        return r_ref.at[side, pl.ds(pl.multiple_of(j * 256 + zp * 64, 64), 64), :]

    own = [pltpu.make_async_copy(piece(0, z, t), columns(x, z, t), own_sem.at[t]) for t in range(2)]
    for cp in own:
        cp.start()
    pl.semaphore_wait(barrier, len(dests))

    for j, zp, d in dests:
        for t in range(2):
            rcopy(
                piece(j, zp, t), columns(x, z, t), ss.at[j, d, t], rs.at[j, z, t], (g, xb[j] * NZ + zp)
            ).start()
    for j, zp, d in dests:
        for t in range(2):
            rcopy(
                piece(j, zp, t), columns(xb[j], zp, t), ss.at[j, d, t], rs.at[j, zp, t],
                (g, xb[j] * NZ + zp),
            ).wait_recv()
    for cp in own:
        cp.wait()
    for j, zp, d in dests:
        for t in range(2):
            rcopy(
                piece(j, zp, t), columns(x, z, t), ss.at[j, d, t], rs.at[j, z, t], (g, xb[j] * NZ + zp)
            ).wait_send()


def deliver(finished):
    dma = pltpu.SemaphoreType.DMA
    return pl.pallas_call(
        deliver_kernel,
        out_shape=jax.ShapeDtypeStruct((64, 16 * PDEV), jnp.bfloat16),
        in_specs=[pl.BlockSpec(memory_space=pl.ANY)],
        out_specs=pl.BlockSpec(memory_space=pl.ANY),
        scratch_shapes=[dma((2,)), dma((2, NZ, 2)), dma((2, NZ, 2))],
        compiler_params=pltpu.CompilerParams(collective_id=1, has_side_effects=True),
        name="deliver",
    )(finished)


def shards(integral_tiles, row_blocks, col_blocks, aux_blocks, tile_counts, occ_coeffs, vir_coeffs):
    halves, vir, meta = spread(
        row_blocks.reshape(KMAX),
        integral_tiles.reshape(KMAX, PB, BLK, BLK),
        col_blocks.reshape(1, KMAX),
        aux_blocks.reshape(1, KMAX),
        tile_counts,
        occ_coeffs,
        vir_coeffs.reshape(4, BLK, V),
    )
    finished = contract(meta, halves, vir)
    return deliver(finished).astype(jnp.float32)


def solution(mesh):
    in_specs = (
        P("grp", "aux", None, None, None, None),
        P("grp", "aux", None),
        P("grp", "aux", None),
        P("grp", "aux", None),
        P("grp", "aux"),
        P(None, "grp"),
        P("grp", None),
    )
    out_specs = P(("grp", "aux"), None)
    return jax.shard_map(shards, mesh=mesh, in_specs=in_specs, out_specs=out_specs, check_vma=False)
```

time: 494 us -> 72.1 us (0.15)
  blocking collectives: 208 us -> 0 us
  waiting for transfers between devices: 89.2 us -> 0 us
  local copies, waits for them, and re-layouts: 90.4 us -> 4.84 us
  Pallas kernels: 0 us -> 63.7 us
  matrix products: 32.6 us -> 0 us
  loops' own time: 30.3 us -> 0 us
  other arithmetic: 27.9 us -> 2.68 us
  between operations: 13.4 us -> 0.7 us
    all_to_all x1 -> x0, blocking collectives: 194 us -> none  [shards(): lax.all_to_all(reordered, 'aux', split_axis=0, concat_axis=1, tiled=True)]
    reduce_scatter x1 -> x0, waiting for transfers between devices: 89.2 us -> none  [shards(): lax.psum_scatter(regrouped, 'grp', scatter_dimension=0, tiled=True)]
    pallas_call x0 -> x3, Pallas kernels: none -> 63.7 us  [the longest x1 38.7 us: spread(): pl.pallas_call(spread_kernel, out_shape=(jax.ShapeDtypeStruct((2, CH, G,...]
    dot_general x24 -> x0, matrix products: 32.6 us -> none  [the longest x12 17.6 us: tile_term(): jnp.einsum('im,pmn->ipn', occ_block, tile, preferred_element_type=jnp.flo...]
    another operation x1 -> x0, loops' own time: 30.3 us -> none  [shards(): partial_value = lax.fori_loop(0, KMAX, padded_step, partial_value)]
    dynamic_update_slice x12 -> x0, other arithmetic: 27.9 us -> none  [add_tile(): lax.dynamic_update_slice_in_dim(partial_value, current + weight * term, s...]
    dynamic_slice x36 -> x0, local copies, waits for them, and re-layouts: 22.2 us -> none  [the longest x12 7.4 us: add_tile(): my_rows[slot]]
    all_to_all x1 -> x0, local copies, waits for them, and re-layouts: 17.6 us -> none  [shards(): lax.all_to_all(reordered, 'aux', split_axis=0, concat_axis=1, tiled=True)]
  transfers between devices with their start and end apart: 1 -> 0, of which waited for: 1 -> 0; matrix products, arithmetic and copies ran while one was open for 0% -> 0% of each run, Pallas kernels for 0% -> 0%
where the time goes in v1:
time: 72.1 us; the launch traced here: 71.9 us
  Pallas kernels  63.7 us (88%)
  local copies, waits for them, and re-layouts  4.84 us (7%)
  other arithmetic  2.68 us (4%)
    pallas_call x1, Pallas kernels, spread(): pl.pallas_call(spread_kernel, out_shape=(jax.ShapeDtypeStruct((2, CH, G,...  38.7 us
    pallas_call x1, Pallas kernels, deliver(): pl.pallas_call(deliver_kernel, out_shape=jax.ShapeDtypeStruct((64, 16 * P...  17 us
    pallas_call x1, Pallas kernels, contract(): pl.pallas_call(contract_kernel, out_shape=jax.ShapeDtypeStruct((2, 512, P...  7.89 us
    unnamed x12, local copies, waits for them, and re-layouts  4.84 us
    convert_element_type x1, other arithmetic, shards(): return deliver(finished).astype(jnp.float32)  2.68 us

profile of v1, /device:TPU:0, one launch (start us, length us, event | category | flops | bytes accessed | tf_op | source)
XLA Modules:
  0.0 71.9 jit_solution(3700691826777126310)
XLA Ops:
  0.7 0.0 copy-start.1
  0.7 1.2 %copy-done.1 = bf16[512,1024]{1,0:T(8,128)(2,1)S(1)} copy-done((bf16[512,1024]{1,0:T(8,128)(2,1)S(1)}, bf16[512,1024]{1,0:T(8,128)(2,1)}, u32[]{:S(2)}) %copy-start.1) | copy-done | bytes 1048600
  1.9 0.0 copy-start.2
  1.9 0.7 copy-done.2
  2.6 0.0 copy-start.3
  2.6 0.7 copy-done.3
  3.2 0.0 copy-start.4
  3.2 0.7 copy-done.4
  3.9 0.0 copy-start.5
  3.9 0.7 copy-done.5
  4.5 38.7 %spread.1 = (bf16[2,4,8,3,32,128]{5,4,3,2,1,0:T(8,128)(2,1)S(1)}, bf16[8,4,2,128,256]{4,3,2,1,0:T(8,128)(2,1)S(1)}, s32[2,8,8,128]{3,2,1,0:T(8,128)S(1)}) custom-call(s32[12]{0:T(128)S(1)} %bitcast.6, bf16[12,32,128,128]{3,2,1,0:T(8,128)(2,1)} %bitcast.9, s32[1,12]{1,0:T(1,128)S(1)} %bitcast.7, s32[1,12]{1,0:T(1,128)S(1)} %bitcast.8, ...), custom_call_target="tpu_custom_call" | custom-call | tf_op jit(solution)/shard_map/spread/pallas_call | solution.py:215
  43.3 7.9 %contract.1.r_ref = bf16[2,512,512]{2,1,0:T(8,128)(2,1)S(1)} custom-call(s32[2,8,8,128]{3,2,1,0:T(8,128)S(1)} %get-tuple-element.8.m_ref, bf16[2,4,8,3,32,128]{5,4,3,2,1,0:T(8,128)(2,1)S(1)} %get-tuple-element.9.h_ref, bf16[8,4,2,128,256]{4,3,2,1,0:T(8,128)(2,1)S(1)} %get-tuple-element.10.v_ref), custom_call_target="tpu_custom_call" | custom-call | tf_op jit(solution)/shard_map/contract/pallas_call | solution.py:272
  51.2 0.0 copy-start
  51.2 1.0 %copy-done = bf16[2,512,512]{2,1,0:T(8,128)(2,1)} copy-done((bf16[2,512,512]{2,1,0:T(8,128)(2,1)}, bf16[2,512,512]{2,1,0:T(8,128)(2,1)S(1)}, u32[]{:S(2)}) %copy-start) | copy-done | bytes 1048600
  52.2 17.0 %deliver.1 = bf16[64,8192]{1,0:T(8,128)(2,1)} custom-call(bf16[2,512,512]{2,1,0:T(8,128)(2,1)} %copy-done), custom_call_target="tpu_custom_call" | custom-call | tf_op jit(solution)/shard_map/deliver/pallas_call | solution.py:334
  69.2 2.7 %convert_element_type.3 = f32[64,8192]{1,0:T(8,128)} convert(bf16[64,8192]{1,0:T(8,128)(2,1)} %deliver.1) | non-fusion elementwise | flops 524288 | bytes 3145728 | tf_op jit(solution)/shard_map/convert_element_type | solution.py:356
Async XLA Ops:
  0.7 1.2 %copy-start.1 = (bf16[512,1024]{1,0:T(8,128)(2,1)S(1)}, bf16[512,1024]{1,0:T(8,128)(2,1)}, u32[]{:S(2)}) copy-start(bf16[512,1024]{1,0:T(8,128)(2,1)} %param.13) | copy-start | bytes 3145732
  1.9 0.7 copy-start.2
  2.6 0.7 copy-start.3
  3.2 0.7 copy-start.4
  3.9 0.7 copy-start.5
  51.2 1.0 %copy-start = (bf16[2,512,512]{2,1,0:T(8,128)(2,1)}, bf16[2,512,512]{2,1,0:T(8,128)(2,1)S(1)}, u32[]{:S(2)}) copy-start(bf16[2,512,512]{2,1,0:T(8,128)(2,1)S(1)} %contract.1.r_ref) | copy-start | bytes 3145732

commit v2 on v1

v2 whole, which is shorter than its diff:
```python
import functools

import jax
import jax.numpy as jnp
from jax import lax
from jax.experimental import pallas as pl
from jax.experimental.pallas import tpu as pltpu
from jax.sharding import PartitionSpec as P

O = 8
V = 1024
BLK = 128
PB = 32
PDEV = 512
KMAX = 12
G = 8
NZ = 4
CH = 4
CT = KMAX // CH
MESH = pl.DeviceIdType.MESH


def rcopy(src, dst, ssem, rsem, dev):
    return pltpu.make_async_remote_copy(
        src_ref=src, dst_ref=dst, send_sem=ssem, recv_sem=rsem, device_id=dev, device_id_type=MESH
    )


def where_am_i():
    g = lax.axis_index("grp")
    a = lax.axis_index("aux")
    return g, a, lax.div(g, 2), lax.rem(g, 2), lax.div(a, NZ), lax.rem(a, NZ)


def mate_x(x, c):
    odd = lax.rem(x, 2)
    return lax.rem(x + 4 + (1 - 2 * odd) * (1 - 2 * c), 4)


def whole_kernel(
    rows_ref, tiles_ref, cols_ref, aux_ref, count_ref, occ_ref, vir_ref,
    o_ref,
    h_ref, v_ref, m_ref, run, done, tab_v, tab,
    rows_s, cols_v, aux_v, count_v, occ_v, tile_v, occ_all, meta_own, stage, hbuf,
    in_sem, tile_sem, own_sem,
    occ_ss, occ_rs, meta_ss, meta_rs, mx_sem,
    h_ss, h_rs, hx_ss, hx_rs,
    vy_ss, vy_rs, vz_ss, vz_rs, vf_ss, vf_rs, vo_ss, vo_rs, vs_ss, vs_rs,
    tab_sem, o_own, o_ss, o_rs,
):
    g, a, y, c, x, z = where_am_i()
    xm = mate_x(x, c)
    mate = (g, xm * NZ + z)
    twin = (2 * y + 1 - c, a)
    xb = (x, lax.rem(x + 2, 4))

    small = [
        pltpu.make_async_copy(src, dst, in_sem.at[n])
        for n, (src, dst) in enumerate((
            (occ_ref, occ_v), (cols_ref, cols_v), (aux_ref, aux_v), (count_ref, count_v), (rows_ref, rows_s)
        ))
    ]
    for cp in small:
        cp.start()

    peers = [lax.rem(g + d, G) for d in range(1, G)]
    ypeers = [2 * lax.rem(y + d, 4) + c for d in (1, 3, 2)]
    zpeers = [lax.rem(z + d, NZ) for d in (1, 3)]
    far_z = lax.rem(z + 2, NZ)
    dests = [(j, lax.rem(z + d, NZ), d) for d in range(NZ) for j in range(2) if (d, j) != (0, 0)]

    barrier = pltpu.get_barrier_semaphore()
    for p in peers:
        pl.semaphore_signal(barrier, inc=1, device_id=(p, a), device_id_type=MESH)
    pl.semaphore_signal(barrier, inc=1, device_id=mate, device_id_type=MESH)
    for j, zp, d in dests:
        pl.semaphore_signal(barrier, inc=1, device_id=(g, xb[j] * NZ + zp), device_id_type=MESH)

    def tile_copy(k):
        return pltpu.make_async_copy(tiles_ref.at[k], tile_v.at[k], tile_sem.at[k])

    for k in range(KMAX):
        tile_copy(k).start()

    def vir_cols(j):
        return vir_ref.at[:, :, pl.ds(pl.multiple_of(xb[j] * 256, 256), 256)]

    v_own = [pltpu.make_async_copy(vir_cols(j), v_ref.at[g, :, j], own_sem.at[j]) for j in range(2)]
    for cp in v_own:
        cp.start()

    for cp in small:
        cp.wait()
    for b in range(4):
        occ_all[g, b] = occ_v[:, b * BLK:(b + 1) * BLK]
    meta_own[...] = jnp.zeros_like(meta_own)
    kept = lax.broadcasted_iota(jnp.int32, (1, KMAX), 1) < count_v[...]
    meta_own[0:1, 0:KMAX] = jnp.where(kept, aux_v[...] + 1, 0)
    meta_own[1:2, 0:KMAX] = cols_v[...]
    meta_own[...] = pltpu.roll(meta_own[...], KMAX * g, 1)
    m_own = pltpu.make_async_copy(meta_own, m_ref.at[0, g], own_sem.at[2])
    m_own.start()

    pl.semaphore_wait(barrier, 8 + len(dests))

    def occ_copy(src, d, dev):
        return rcopy(occ_all.at[src], occ_all.at[src], occ_ss.at[d], occ_rs.at[src], dev)

    def meta_copy(src, d, dev):
        return rcopy(meta_own, m_ref.at[0, src], meta_ss.at[d], meta_rs.at[src], dev)

    for d, p in enumerate(peers):
        occ_copy(g, d, (p, a)).start()

    def vy_copy(src, d, j, dev):
        return rcopy(
            vir_ref.at[z, :, pl.ds(pl.multiple_of(xb[j] * 256, 256), 256)],
            v_ref.at[src, z, j], vy_ss.at[d, j], vy_rs.at[lax.div(src, 2), j], dev,
        )

    for d, p in enumerate(ypeers):
        for j in range(2):
            vy_copy(g, d, j, (p, a)).start()
    for d, p in enumerate(peers):
        meta_copy(g, d, (p, a)).start()

    def vo_copy(src, j):
        return rcopy(vir_cols(j), v_ref.at[src, :, j], vo_ss.at[j], vo_rs.at[j], twin)

    for j in range(2):
        vo_copy(g, j).start()

    for d, p in enumerate(peers):
        occ_copy(p, d, (p, a)).wait_recv()

    def compute(chunk):
        def one(t, carry):
            k = chunk * CT + t
            tile_copy(k).wait()
            row = rows_s[0, k]
            occ = occ_all[lax.div(row, 4), lax.rem(row, 4)]
            for pp in range(PB // 2):
                rhs = jnp.concatenate([tile_v[k, 2 * pp], tile_v[k, 2 * pp + 1]], axis=1)
                out = jnp.dot(occ, rhs, preferred_element_type=jnp.float32)
                stage[16 * pp:16 * pp + 8, :] = out[:, :BLK]
                stage[16 * pp + 8:16 * pp + 16, :] = out[:, BLK:]
            for i in range(O):
                hbuf[i, chunk, t] = stage[pl.ds(i, PB, stride=O), :].astype(jnp.bfloat16)
            return carry

        lax.fori_loop(0, CT, one, 0)

    def h_copy(dst_g, src, chunk, d, dev):
        return rcopy(
            hbuf.at[dst_g, chunk], h_ref.at[0, chunk, src], h_ss.at[chunk, d], h_rs.at[chunk, src], dev
        )

    def h_own(chunk):
        return pltpu.make_async_copy(hbuf.at[g, chunk], h_ref.at[0, chunk, g], own_sem.at[3 + chunk])

    def hx_copy(chunk):
        return rcopy(h_ref.at[0, chunk], h_ref.at[1, chunk], hx_ss.at[chunk], hx_rs.at[chunk], mate)

    def mx_copy():
        return rcopy(m_ref.at[0], m_ref.at[1], mx_sem.at[0], mx_sem.at[1], mate)

    def forward_h(chunk):
        h_own(chunk).wait()
        for d, p in enumerate(peers):
            h_copy(p, p, chunk, d, (p, a)).wait_recv()
        hx_copy(chunk).start()

    def vz_copy(src, src_z, d, e, dev):
        return rcopy(
            v_ref.at[src, src_z], v_ref.at[src, src_z], vz_ss.at[d, e],
            vz_rs.at[lax.div(src, 2), src_z], dev,
        )

    def vf_copy(src, src_z, d, e, dev):
        return rcopy(
            v_ref.at[src, src_z, e], v_ref.at[src, src_z, e], vf_ss.at[d, e],
            vf_rs.at[lax.div(src, 2), e], dev,
        )

    def vs_copy(src, d):
        return rcopy(v_ref.at[src], v_ref.at[src], vs_ss.at[d], vs_rs.at[lax.div(src, 2)], twin)

    def start_z(d):
        p = ypeers[d]
        for j in range(2):
            vy_copy(p, d, j, (p, a)).wait_recv()
        for e, zp in enumerate(zpeers):
            vz_copy(p, z, d, e, (g, x * NZ + zp)).start()

    def pass_z(d):
        p = ypeers[d]
        for e in range(2):
            vz_copy(p, zpeers[1 - e], d, e, (g, x * NZ + zpeers[1 - e])).wait_recv()
            vf_copy(p, zpeers[1 - e], d, e, (g, x * NZ + zpeers[e])).start()

    def finish_z(d):
        p = ypeers[d]
        for e in range(2):
            vf_copy(p, far_z, d, e, (g, x * NZ + zpeers[e])).wait_recv()
        vs_copy(p, d).start()

    for chunk in range(CH):
        compute(chunk)
        for d, p in enumerate(peers):
            h_copy(p, g, chunk, d, (p, a)).start()
        h_own(chunk).start()
        if chunk == 1:
            start_z(0)
            start_z(1)
        if chunk == 2:
            start_z(2)
        if chunk == 3:
            m_own.wait()
            for d, p in enumerate(peers):
                meta_copy(p, d, (p, a)).wait_recv()
            mx_copy().start()
    forward_h(0)
    pass_z(0)
    forward_h(1)
    pass_z(1)
    forward_h(2)
    pass_z(2)
    forward_h(3)
    for d in range(3):
        finish_z(d)

    def chain(side):
        total = m_ref[side, 0]
        for p in range(1, G):
            total += m_ref[side, p]
        key = jnp.broadcast_to(total[0:1, :], (128, 128))
        key_t = key.T
        slot = lax.broadcasted_iota(jnp.int32, (128, 128), 0)
        lane = lax.broadcasted_iota(jnp.int32, (128, 128), 1)
        before = jnp.where((key_t == key) & (slot < lane), slot + 1, 0)
        last = jnp.where(key_t == lane + 1, slot + 1, 0)
        tab_v[side, 0:1, :] = jnp.max(before, axis=0, keepdims=True)
        tab_v[side, 1:2, :] = total[1:2, :]
        tab_v[side, 2:3, :] = jnp.max(last, axis=0, keepdims=True)
        return pltpu.make_async_copy(tab_v.at[side], tab.at[side], tab_sem.at[side])

    def contract(side):
        def group(p, carry):
            for k in range(KMAX):
                t = p * KMAX + k
                col = tab[side, 1, t]
                prev = tab[side, 0, t]
                half = h_ref[side, k // CT, p, k % CT]
                for j in range(2):
                    term = jnp.dot(half, v_ref[p, col, j], preferred_element_type=jnp.float32)
                    run[t + 1, j] = term + run[prev, j]
            return carry

        lax.fori_loop(0, G, group, 0)

        def flip(q, carry):
            at = [tab[side, 2, 4 * q + b] for b in range(4)]
            for j in range(2):
                block = jnp.concatenate([run[at[b], j] for b in range(4)], axis=0)
                done[side, q, j] = block.T.astype(jnp.bfloat16)
            return carry

        lax.fori_loop(0, PDEV // BLK, flip, 0)

    def columns(x_src, z_src, side, q):
        x_aux = (x_src, mate_x(x_src, c))[side]
        first = (x_aux * NZ + z_src) * PDEV + q * BLK
        return o_ref.at[:, pl.ds(pl.multiple_of(first, BLK), BLK)]

    def piece(j, zp, side, q):
        return done.at[side, q, j, pl.ds(pl.multiple_of(zp * 64, 64), 64), :]

    def out_copy(j, zp, d, side, q, x_src, z_src):
        return rcopy(
            piece(j, zp, side, q), columns(x_src, z_src, side, q), o_ss.at[j, d, side, q],
            o_rs.at[j, z_src, side, q], (g, xb[j] * NZ + zp),
        )

    def own_copy(side, q):
        return pltpu.make_async_copy(piece(0, z, side, q), columns(x, z, side, q), o_own.at[side, q])

    def send_out(side):
        for j, zp, d in dests:
            for q in range(4):
                out_copy(j, zp, d, side, q, x, z).start()
        for q in range(4):
            own_copy(side, q).start()

    for j in range(2):
        vo_copy(2 * y + 1 - c, j).wait_recv()
        v_own[j].wait()
    mx_copy().wait_recv()
    tables = [chain(side) for side in range(2)]
    for cp in tables:
        cp.start()
    run[0] = jnp.zeros_like(run[0])
    for cp in tables:
        cp.wait()
    for d in range(1, 4):
        vs_copy(2 * lax.rem(y + d, 4) + 1 - c, d - 1).wait_recv()
    contract(0)
    send_out(0)
    for chunk in range(CH):
        hx_copy(chunk).wait_recv()
    contract(1)
    send_out(1)

    for side in range(2):
        for j, zp, d in dests:
            for q in range(4):
                out_copy(j, zp, d, side, q, xb[j], zp).wait_recv()
        for q in range(4):
            own_copy(side, q).wait()
    for side in range(2):
        for j, zp, d in dests:
            for q in range(4):
                out_copy(j, zp, d, side, q, x, z).wait_send()

    for d, p in enumerate(peers):
        occ_copy(g, d, (p, a)).wait_send()
        meta_copy(g, d, (p, a)).wait_send()
        for chunk in range(CH):
            h_copy(p, g, chunk, d, (p, a)).wait_send()
    for d, p in enumerate(ypeers):
        for j in range(2):
            vy_copy(g, d, j, (p, a)).wait_send()
        for e in range(2):
            vz_copy(p, z, d, e, (g, x * NZ + zpeers[e])).wait_send()
            vf_copy(p, zpeers[1 - e], d, e, (g, x * NZ + zpeers[e])).wait_send()
        vs_copy(p, d).wait_send()
    for j in range(2):
        vo_copy(g, j).wait_send()
    mx_copy().wait_send()
    for chunk in range(CH):
        hx_copy(chunk).wait_send()


def whole(rows, tiles, cols, aux, count, occ, vir):
    anywhere = pl.BlockSpec(memory_space=pl.ANY)
    dma = pltpu.SemaphoreType.DMA
    return pl.pallas_call(
        whole_kernel,
        out_shape=jax.ShapeDtypeStruct((64, 16 * PDEV), jnp.bfloat16),
        in_specs=[anywhere] * 7,
        out_specs=anywhere,
        scratch_shapes=[
            pltpu.VMEM((2, CH, G, CT, PB, BLK), jnp.bfloat16),
            pltpu.VMEM((G, 4, 2, BLK, 256), jnp.bfloat16),
            pltpu.VMEM((2, G, 8, 128), jnp.int32),
            pltpu.VMEM((1 + G * KMAX, 2, PB, 256), jnp.float32),
            pltpu.VMEM((2, 4, 2, 256, BLK), jnp.bfloat16),
            pltpu.VMEM((2, 8, 128), jnp.int32),
            pltpu.SMEM((2, 8, 128), jnp.int32),
            pltpu.SMEM((1, KMAX), jnp.int32),
            pltpu.VMEM((1, KMAX), jnp.int32),
            pltpu.VMEM((1, KMAX), jnp.int32),
            pltpu.VMEM((1, 1), jnp.int32),
            pltpu.VMEM((O, 4 * BLK), jnp.bfloat16),
            pltpu.VMEM((KMAX, PB, BLK, BLK), jnp.bfloat16),
            pltpu.VMEM((G, 4, O, BLK), jnp.bfloat16),
            pltpu.VMEM((8, 128), jnp.int32),
            pltpu.VMEM((PB * O, BLK), jnp.float32),
            pltpu.VMEM((O, CH, CT, PB, BLK), jnp.bfloat16),
            dma((5,)), dma((KMAX,)), dma((3 + CH,)),
            dma((7,)), dma((G,)), dma((7,)), dma((G,)), dma((2,)),
            dma((CH, 7)), dma((CH, G)), dma((CH,)), dma((CH,)),
            dma((3, 2)), dma((4, 2)), dma((3, 2)), dma((4, NZ)), dma((3, 2)), dma((4, 2)),
            dma((2,)), dma((2,)), dma((3,)), dma((4,)),
            dma((2,)), dma((2, 4)), dma((2, NZ, 2, 4)), dma((2, NZ, 2, 4)),
        ],
        compiler_params=pltpu.CompilerParams(
            collective_id=0, has_side_effects=True, vmem_limit_bytes=60 * 1024 * 1024
        ),
        name="whole",
    )(rows, tiles, cols, aux, count, occ, vir)


def shards(integral_tiles, row_blocks, col_blocks, aux_blocks, tile_counts, occ_coeffs, vir_coeffs):
    result = whole(
        row_blocks.reshape(1, KMAX),
        integral_tiles.reshape(KMAX, PB, BLK, BLK),
        col_blocks.reshape(1, KMAX),
        aux_blocks.reshape(1, KMAX),
        tile_counts,
        occ_coeffs,
        vir_coeffs.reshape(4, BLK, V),
    )
    return result.astype(jnp.float32)


def solution(mesh):
    in_specs = (
        P("grp", "aux", None, None, None, None),
        P("grp", "aux", None),
        P("grp", "aux", None),
        P("grp", "aux", None),
        P("grp", "aux"),
        P(None, "grp"),
        P("grp", None),
    )
    out_specs = P(("grp", "aux"), None)
    return jax.shard_map(shards, mesh=mesh, in_specs=in_specs, out_specs=out_specs, check_vma=False)
```

time: 72.1 us -> 55.2 us (0.77)
  the two profiles are of different devices: /device:TPU:0 before, /device:TPU:1 now
where the time goes in v2:
time: 55.2 us; the launch traced here: 55 us
  Pallas kernels  51.7 us (94%)
  other arithmetic  2.68 us (5%)
  between operations  0.66 us (1%)
    pallas_call x1, Pallas kernels, whole(): pl.pallas_call(whole_kernel, out_shape=jax.ShapeDtypeStruct((64, 16 * PDE...  51.7 us
    convert_element_type x1, other arithmetic, shards(): return result.astype(jnp.float32)  2.68 us

profile of v2, /device:TPU:1, one launch (start us, length us, event | category | flops | bytes accessed | tf_op | source)
XLA Modules:
  0.0 55.0 jit_solution(2191260050017750251)
XLA Ops:
  0.7 51.7 %whole.1 = bf16[64,8192]{1,0:T(8,128)(2,1)} custom-call(s32[1,12]{1,0:T(1,128)} %bitcast.7, bf16[12,32,128,128]{3,2,1,0:T(8,128)(2,1)} %bitcast.5, s32[1,12]{1,0:T(1,128)} %bitcast.8, s32[1,12]{1,0:T(1,128)} %bitcast.9, s32[1,1]{1,0:T(1,128)S(6)} %copy.8.count_ref, bf16[8,512]{1,0:T(8,128)(2,1)} %occ_ref.1, bf16[4,128,1024]{2,1,0:T(8,128)(2,1)} %bitcast.6), custom_call_target="tpu_custom_call" | custom-call | tf_op jit(solution)/shard_map/whole/pallas_call | solution.py:346
  52.4 2.7 %convert_element_type.3 = f32[64,8192]{1,0:T(8,128)} convert(bf16[64,8192]{1,0:T(8,128)(2,1)} %whole.1) | non-fusion elementwise | flops 524288 | bytes 3145728 | tf_op jit(solution)/shard_map/convert_element_type | solution.py:393

commit v3 on v2

v3 whole, which is shorter than its diff:
```python
import functools

import jax
import jax.numpy as jnp
from jax import lax
from jax.experimental import pallas as pl
from jax.experimental.pallas import tpu as pltpu
from jax.sharding import PartitionSpec as P

O = 8
V = 1024
BLK = 128
PB = 32
PDEV = 512
KMAX = 12
G = 8
NZ = 4
CH = 4
CT = KMAX // CH
MESH = pl.DeviceIdType.MESH


def rcopy(src, dst, ssem, rsem, dev):
    return pltpu.make_async_remote_copy(
        src_ref=src, dst_ref=dst, send_sem=ssem, recv_sem=rsem, device_id=dev, device_id_type=MESH
    )


def where_am_i():
    g = lax.axis_index("grp")
    a = lax.axis_index("aux")
    return g, a, lax.div(g, 2), lax.rem(g, 2), lax.div(a, NZ), lax.rem(a, NZ)


def mate_x(x, c):
    odd = lax.rem(x, 2)
    return lax.rem(x + 4 + (1 - 2 * odd) * (1 - 2 * c), 4)


def whole_kernel(
    rows_ref, tiles_ref, cols_ref, aux_ref, count_ref, occ_ref, vir_ref,
    o_ref,
    h_ref, vf_ref, vn_ref, m_ref, run, done, tab_v, tab,
    rows_s, cols_v, aux_v, count_v, occ_v, tile_v, occ_all, meta_own, stage, hbuf,
    in_sem, tile_sem, own_sem,
    occ_ss, occ_rs, meta_ss, meta_rs, mx_sem,
    h_ss, h_rs, hx_ss, hx_rs,
    vy_ss, vy_rs, vz_ss, vz_rs, zf_ss, zf_rs, vo_ss, vo_rs, vs_ss, vs_rs,
    tab_sem, o_own, o_ss, o_rs, ready,
):
    g, a, y, c, x, z = where_am_i()
    xm = mate_x(x, c)
    mate = (g, xm * NZ + z)
    twin = (2 * y + 1 - c, a)
    xb = (lax.rem(x + 2, 4), x)
    v_ref = (vf_ref, vn_ref)

    small = [
        pltpu.make_async_copy(src, dst, in_sem.at[n])
        for n, (src, dst) in enumerate((
            (occ_ref, occ_v), (cols_ref, cols_v), (aux_ref, aux_v), (count_ref, count_v), (rows_ref, rows_s)
        ))
    ]
    for cp in small:
        cp.start()

    peers = [2 * lax.rem(y + d, 4) + lax.rem(c + e, 2) for d, e in ((0, 1), (1, 0), (3, 0), (1, 1), (3, 1), (2, 0), (2, 1))]
    around = [2 * lax.rem(y + d, 4) + c for d in range(4)]
    quarter = [lax.rem(z + d, NZ) for d in range(4)]
    block = (around[3], around[1], around[2])
    ahead = (1, 3)
    dests = [(j, quarter[d], d) for j in range(2) for d in range(NZ) if (d, j) != (0, 1)]

    barrier = pltpu.get_barrier_semaphore()
    for p in peers:
        pl.semaphore_signal(barrier, inc=1, device_id=(p, a), device_id_type=MESH)
    below = (g, lax.rem(x + 3, 4) * NZ + z)
    above = (g, lax.rem(x + 1, 4) * NZ + z)
    for dev in (below, above):
        pl.semaphore_signal(barrier, inc=1, device_id=dev, device_id_type=MESH)
    for zp in quarter[1:]:
        pl.semaphore_signal(barrier, inc=1, device_id=(g, x * NZ + zp), device_id_type=MESH)

    def tile_copy(k):
        return pltpu.make_async_copy(tiles_ref.at[k], tile_v.at[k], tile_sem.at[k])

    for k in range(KMAX):
        tile_copy(k).start()

    def vir_cols(j):
        return vir_ref.at[:, :, pl.ds(pl.multiple_of(xb[j] * 256, 256), 256)]

    v_own = [pltpu.make_async_copy(vir_cols(j), v_ref[j].at[g], own_sem.at[j]) for j in range(2)]
    for cp in v_own:
        cp.start()

    for cp in small:
        cp.wait()
    for b in range(4):
        occ_all[g, b] = occ_v[:, b * BLK:(b + 1) * BLK]
    meta_own[...] = jnp.zeros_like(meta_own)
    kept = lax.broadcasted_iota(jnp.int32, (1, KMAX), 1) < count_v[...]
    meta_own[0:1, 0:KMAX] = jnp.where(kept, aux_v[...] + 1, 0)
    meta_own[1:2, 0:KMAX] = cols_v[...]
    meta_own[...] = pltpu.roll(meta_own[...], KMAX * g, 1)
    m_own = pltpu.make_async_copy(meta_own, m_ref.at[0, g], own_sem.at[2])
    m_own.start()

    pl.semaphore_wait(barrier, 12)
    pl.semaphore_signal(ready.at[0], inc=1, device_id=below, device_id_type=MESH)

    def occ_copy(src, d, dev):
        return rcopy(occ_all.at[src], occ_all.at[src], occ_ss.at[d], occ_rs.at[src], dev)

    def meta_copy(src, d, dev):
        return rcopy(meta_own, m_ref.at[0, src], meta_ss.at[d], meta_rs.at[src], dev)

    for d, p in enumerate(peers):
        occ_copy(g, d, (p, a)).start()

    def vy_copy(src, b, j):
        return rcopy(
            vir_ref.at[z, :, pl.ds(pl.multiple_of(xb[j] * 256, 256), 256)], v_ref[j].at[src, z],
            vy_ss.at[b, j], vy_rs.at[b, j], (block[(1, 0, 2)[b]], a),
        )

    def half(ref, e):
        return ref.at[64 * e:64 * e + 64, :]

    for j in range(2):
        for b in range(3):
            vy_copy(g, b, j).start()
    for d, p in enumerate(peers):
        meta_copy(g, d, (p, a)).start()

    def vo_copy(src, j):
        return rcopy(vir_cols(j), v_ref[j].at[src], vo_ss.at[j], vo_rs.at[j], twin)

    for j in range(2):
        vo_copy(g, j).start()

    def compute(chunk):
        def one(t, carry):
            k = chunk * CT + t
            tile_copy(k).wait()
            row = rows_s[0, k]
            occ = occ_all[lax.div(row, 4), lax.rem(row, 4)]
            for pp in range(PB // 2):
                rhs = jnp.concatenate([tile_v[k, 2 * pp], tile_v[k, 2 * pp + 1]], axis=1)
                out = jnp.dot(occ, rhs, preferred_element_type=jnp.float32)
                stage[16 * pp:16 * pp + 8, :] = out[:, :BLK]
                stage[16 * pp + 8:16 * pp + 16, :] = out[:, BLK:]
            for i in range(O):
                hbuf[i, chunk, t] = stage[pl.ds(i, PB, stride=O), :].astype(jnp.bfloat16)
            return carry

        lax.fori_loop(0, CT, one, 0)

    def h_copy(dst_g, src, chunk, d, dev):
        return rcopy(
            hbuf.at[dst_g, chunk], h_ref.at[0, chunk, src], h_ss.at[chunk, d], h_rs.at[chunk, src], dev
        )

    def h_own(chunk):
        return pltpu.make_async_copy(hbuf.at[g, chunk], h_ref.at[0, chunk, g], own_sem.at[3 + chunk])

    def hx_copy(chunk, src):
        return rcopy(
            h_ref.at[0, chunk, src], h_ref.at[1, chunk, src], hx_ss.at[chunk, src], hx_rs.at[chunk, src], mate
        )

    def mx_copy():
        return rcopy(m_ref.at[0], m_ref.at[1], mx_sem.at[0], mx_sem.at[1], mate)

    def forward_h(chunk):
        h_own(chunk).wait()
        hx_copy(chunk, g).start()
        for d, p in enumerate(peers):
            h_copy(p, p, chunk, d, (p, a)).wait_recv()
            hx_copy(chunk, p).start()

    def vz_copy(b, q, e, j):
        return rcopy(
            v_ref[j].at[block[b], quarter[q]], v_ref[j].at[block[b], quarter[q]],
            vz_ss.at[b, e, j], vz_rs.at[b, e, j], (g, x * NZ + quarter[ahead[e]]),
        )

    def zf_copy(b, q, e, j):
        rows = half(v_ref[j].at[block[b], quarter[q]], e)
        return rcopy(
            rows, rows, zf_ss.at[b, e, j], zf_rs.at[b, e, j], (g, x * NZ + quarter[ahead[e]])
        )

    def vs_copy(src, b, j):
        return rcopy(v_ref[j].at[src], v_ref[j].at[src], vs_ss.at[b, j], vs_rs.at[b, j], twin)

    def start_z(b, j):
        vy_copy(block[b], b, j).wait_recv()
        for e in range(2):
            vz_copy(b, 0, e, j).start()

    def pass_z(b, j):
        for e in range(2):
            vz_copy(b, ahead[1 - e], e, j).wait_recv()
            zf_copy(b, ahead[1 - e], e, j).start()

    def finish_z(b, j):
        for e in range(2):
            zf_copy(b, 2, e, j).wait_recv()
        vs_copy(block[b], b, j).start()

    start_z(0, 0)
    start_z(1, 0)
    for d, p in enumerate(peers):
        occ_copy(p, d, (p, a)).wait_recv()
    for chunk in range(CH):
        compute(chunk)
        for d, p in enumerate(peers):
            h_copy(p, g, chunk, d, (p, a)).start()
        h_own(chunk).start()
        if chunk == 0:
            start_z(2, 0)
            pl.semaphore_wait(ready.at[0], 1)
            pl.semaphore_signal(ready.at[1], inc=1, device_id=below, device_id_type=MESH)
        if chunk == 1:
            start_z(0, 1)
            start_z(1, 1)
        if chunk == 2:
            start_z(2, 1)
        if chunk == 3:
            m_own.wait()
            for d, p in enumerate(peers):
                meta_copy(p, d, (p, a)).wait_recv()
            mx_copy().start()
    def chain(side):
        total = m_ref[side, 0]
        for p in range(1, G):
            total += m_ref[side, p]
        key = jnp.broadcast_to(total[0:1, :], (128, 128))
        key_t = key.T
        slot = lax.broadcasted_iota(jnp.int32, (128, 128), 0)
        lane = lax.broadcasted_iota(jnp.int32, (128, 128), 1)
        before = jnp.where((key_t == key) & (slot < lane), slot + 1, 0)
        last = jnp.where(key_t == lane + 1, slot + 1, 0)
        tab_v[side, 0:1, :] = jnp.max(before, axis=0, keepdims=True)
        tab_v[side, 1:2, :] = total[1:2, :]
        tab_v[side, 2:3, :] = jnp.max(last, axis=0, keepdims=True)
        return pltpu.make_async_copy(tab_v.at[side], tab.at[side], tab_sem.at[side])

    def contract(side, j):
        def group(p, carry):
            for k in range(KMAX):
                t = p * KMAX + k
                piece = h_ref[side, k // CT, p, k % CT]
                term = jnp.dot(piece, v_ref[j][p, tab[side, 1, t]], preferred_element_type=jnp.float32)
                run[t + 1] = term + run[tab[side, 0, t]]
            return carry

        lax.fori_loop(0, G, group, 0)
        for q in range(4):
            blocks = [run[tab[side, 2, 4 * q + b]] for b in range(4)]
            done[side, j, :, q * BLK:(q + 1) * BLK] = (
                jnp.concatenate(blocks, axis=0).T.astype(jnp.bfloat16)
            )

    def columns(x_src, z_src, side):
        first = ((x_src, mate_x(x_src, c))[side] * NZ + z_src) * PDEV
        return o_ref.at[:, pl.ds(pl.multiple_of(first, PDEV), PDEV)]

    def piece_of(j, zp, side):
        return done.at[side, j, pl.ds(pl.multiple_of(zp * 64, 64), 64), :]

    def out_copy(j, d, side, x_src, z_src):
        return rcopy(
            piece_of(j, quarter[d], side), columns(x_src, z_src, side), o_ss.at[j, d, side],
            o_rs.at[j, z_src, side], (g, xb[j] * NZ + quarter[d]),
        )

    def own_copy(side):
        return pltpu.make_async_copy(piece_of(1, z, side), columns(x, z, side), o_own.at[side])

    def send_out(side, j):
        for jj, zp, d in dests:
            if jj == j:
                out_copy(j, d, side, x, z).start()
        if j == 1:
            own_copy(side).start()

    def twins(j):
        vo_copy(2 * y + 1 - c, j).wait_recv()
        v_own[j].wait()
        for b in range(3):
            vs_copy(block[b] + 1 - 2 * c, b, j).wait_recv()

    pass_z(0, 0)
    pass_z(1, 0)
    forward_h(0)
    pass_z(2, 0)
    mx_copy().wait_recv()
    tables = [chain(side) for side in range(2)]
    for cp in tables:
        cp.start()
    run[0] = jnp.zeros_like(run[0])
    finish_z(0, 0)
    finish_z(1, 0)
    forward_h(1)
    finish_z(2, 0)
    pass_z(0, 1)
    pass_z(1, 1)
    forward_h(2)
    pass_z(2, 1)
    forward_h(3)
    for cp in tables:
        cp.wait()
    twins(0)
    contract(0, 0)
    pl.semaphore_wait(ready.at[1], 1)
    send_out(0, 0)
    for b in range(3):
        finish_z(b, 1)
    twins(1)
    contract(0, 1)
    send_out(0, 1)
    for chunk in range(CH):
        for p in range(G):
            hx_copy(chunk, p).wait_recv()
    for j in range(2):
        contract(1, j)
        send_out(1, j)

    for side in range(2):
        for j, zp, d in dests:
            out_copy(j, d, side, xb[j], zp).wait_recv()
        own_copy(side).wait()
    for side in range(2):
        for j, zp, d in dests:
            out_copy(j, d, side, x, z).wait_send()

    for d, p in enumerate(peers):
        occ_copy(g, d, (p, a)).wait_send()
        meta_copy(g, d, (p, a)).wait_send()
        for chunk in range(CH):
            h_copy(p, g, chunk, d, (p, a)).wait_send()
    for j in range(2):
        for e in range(2):
            for b in range(3):
                vz_copy(b, 0, e, j).wait_send()
                zf_copy(b, ahead[1 - e], e, j).wait_send()
        for b in range(3):
            vy_copy(g, b, j).wait_send()
            vs_copy(block[b], b, j).wait_send()
    for j in range(2):
        vo_copy(g, j).wait_send()
    mx_copy().wait_send()
    for chunk in range(CH):
        for p in range(G):
            hx_copy(chunk, p).wait_send()


def whole(rows, tiles, cols, aux, count, occ, vir):
    anywhere = pl.BlockSpec(memory_space=pl.ANY)
    dma = pltpu.SemaphoreType.DMA
    return pl.pallas_call(
        whole_kernel,
        out_shape=jax.ShapeDtypeStruct((64, 16 * PDEV), jnp.bfloat16),
        in_specs=[anywhere] * 7,
        out_specs=anywhere,
        scratch_shapes=[
            pltpu.VMEM((2, CH, G, CT, PB, BLK), jnp.bfloat16),
            pltpu.VMEM((G, 4, BLK, 256), jnp.bfloat16),
            pltpu.VMEM((G, 4, BLK, 256), jnp.bfloat16),
            pltpu.VMEM((2, G, 8, 128), jnp.int32),
            pltpu.VMEM((1 + G * KMAX, PB, 256), jnp.float32),
            pltpu.VMEM((2, 2, 256, PDEV), jnp.bfloat16),
            pltpu.VMEM((2, 8, 128), jnp.int32),
            pltpu.SMEM((2, 8, 128), jnp.int32),
            pltpu.SMEM((1, KMAX), jnp.int32),
            pltpu.VMEM((1, KMAX), jnp.int32),
            pltpu.VMEM((1, KMAX), jnp.int32),
            pltpu.VMEM((1, 1), jnp.int32),
            pltpu.VMEM((O, 4 * BLK), jnp.bfloat16),
            pltpu.VMEM((KMAX, PB, BLK, BLK), jnp.bfloat16),
            pltpu.VMEM((G, 4, O, BLK), jnp.bfloat16),
            pltpu.VMEM((8, 128), jnp.int32),
            pltpu.VMEM((PB * O, BLK), jnp.float32),
            pltpu.VMEM((O, CH, CT, PB, BLK), jnp.bfloat16),
            dma((5,)), dma((KMAX,)), dma((3 + CH,)),
            dma((7,)), dma((G,)), dma((7,)), dma((G,)), dma((2,)),
            dma((CH, 7)), dma((CH, G)), dma((CH, G)), dma((CH, G)),
            dma((3, 2)), dma((3, 2)),
            dma((3, 2, 2)), dma((3, 2, 2)), dma((3, 2, 2)), dma((3, 2, 2)),
            dma((2,)), dma((2,)), dma((3, 2)), dma((3, 2)),
            dma((2,)), dma((2,)), dma((2, NZ, 2)), dma((2, NZ, 2)),
            pltpu.SemaphoreType.REGULAR((2,)),
        ],
        compiler_params=pltpu.CompilerParams(
            collective_id=0, has_side_effects=True, vmem_limit_bytes=60 * 1024 * 1024
        ),
        name="whole",
    )(rows, tiles, cols, aux, count, occ, vir)


def shards(integral_tiles, row_blocks, col_blocks, aux_blocks, tile_counts, occ_coeffs, vir_coeffs):
    result = whole(
        row_blocks.reshape(1, KMAX),
        integral_tiles.reshape(KMAX, PB, BLK, BLK),
        col_blocks.reshape(1, KMAX),
        aux_blocks.reshape(1, KMAX),
        tile_counts,
        occ_coeffs,
        vir_coeffs.reshape(4, BLK, V),
    )
    return result.astype(jnp.float32)


def solution(mesh):
    in_specs = (
        P("grp", "aux", None, None, None, None),
        P("grp", "aux", None),
        P("grp", "aux", None),
        P("grp", "aux", None),
        P("grp", "aux"),
        P(None, "grp"),
        P("grp", None),
    )
    out_specs = P(("grp", "aux"), None)
    return jax.shard_map(shards, mesh=mesh, in_specs=in_specs, out_specs=out_specs, check_vma=False)
```

time: 55.2 us -> 51.7 us (0.937)
  the two profiles are of different devices: /device:TPU:1 before, /device:TPU:0 now
where the time goes in v3:
time: 51.7 us; the launch traced here: 51.5 us
  Pallas kernels  48.2 us (93%)
  other arithmetic  2.68 us (5%)
  between operations  0.66 us (1%)
    pallas_call x1, Pallas kernels, whole(): pl.pallas_call(whole_kernel, out_shape=jax.ShapeDtypeStruct((64, 16 * PDE...  48.2 us
    convert_element_type x1, other arithmetic, shards(): return result.astype(jnp.float32)  2.68 us

profile of v3, /device:TPU:0, one launch (start us, length us, event | category | flops | bytes accessed | tf_op | source)
XLA Modules:
  0.0 51.5 jit_solution(17036573962267847222)
XLA Ops:
  0.7 48.2 %whole.1 = bf16[64,8192]{1,0:T(8,128)(2,1)} custom-call(s32[1,12]{1,0:T(1,128)} %bitcast.7, bf16[12,32,128,128]{3,2,1,0:T(8,128)(2,1)} %bitcast.5, s32[1,12]{1,0:T(1,128)} %bitcast.8, s32[1,12]{1,0:T(1,128)} %bitcast.9, s32[1,1]{1,0:T(1,128)S(6)} %copy.8.count_ref, bf16[8,512]{1,0:T(8,128)(2,1)} %occ_ref.1, bf16[4,128,1024]{2,1,0:T(8,128)(2,1)} %bitcast.6), custom_call_target="tpu_custom_call" | custom-call | tf_op jit(solution)/shard_map/whole/pallas_call | solution.py:363
  48.8 2.7 %convert_element_type.3 = f32[64,8192]{1,0:T(8,128)} convert(bf16[64,8192]{1,0:T(8,128)(2,1)} %whole.1) | non-fusion elementwise | flops 524288 | bytes 3145728 | tf_op jit(solution)/shard_map/convert_element_type | solution.py:413

commit v4 on v3

--- a/solution.py
+++ b/solution.py
@@ -69,7 +69,7 @@
     quarter = [lax.rem(z + d, NZ) for d in range(4)]
     block = (around[3], around[1], around[2])
     ahead = (1, 3)
-    dests = [(j, quarter[d], d) for j in range(2) for d in range(NZ) if (d, j) != (0, 1)]
+    dests = [(j, quarter[d], d) for j in range(2) for d in (2, 1, 3, 0) if (d, j) != (0, 1)]
 
     barrier = pltpu.get_barrier_semaphore()
     for p in peers:
@@ -94,10 +94,35 @@
     for cp in v_own:
         cp.start()
 
-    for cp in small:
-        cp.wait()
+    small[0].wait()
     for b in range(4):
         occ_all[g, b] = occ_v[:, b * BLK:(b + 1) * BLK]
+    pl.semaphore_wait(barrier, 12)
+    pl.semaphore_signal(ready.at[0], inc=1, device_id=below, device_id_type=MESH)
+
+    def occ_copy(src, d, dev):
+        return rcopy(occ_all.at[src], occ_all.at[src], occ_ss.at[d], occ_rs.at[src], dev)
+
+    def meta_copy(src, d, dev):
+        return rcopy(meta_own, m_ref.at[0, src], meta_ss.at[d], meta_rs.at[src], dev)
+
+    for d, p in enumerate(peers):
+        occ_copy(g, d, (p, a)).start()
+
+    def vy_copy(src, b, j):
+        return rcopy(
+            vir_ref.at[z, :, pl.ds(pl.multiple_of(xb[j] * 256, 256), 256)], v_ref[j].at[src, z],
+            vy_ss.at[b, j], vy_rs.at[b, j], (block[(1, 0, 2)[b]], a),
+        )
+
+    def half(ref, e):
+        return ref.at[64 * e:64 * e + 64, :]
+
+    for j in range(2):
+        for b in range(3):
+            vy_copy(g, b, j).start()
+    for cp in small[1:]:
+        cp.wait()
     meta_own[...] = jnp.zeros_like(meta_own)
     kept = lax.broadcasted_iota(jnp.int32, (1, KMAX), 1) < count_v[...]
     meta_own[0:1, 0:KMAX] = jnp.where(kept, aux_v[...] + 1, 0)
@@ -105,31 +130,6 @@
     meta_own[...] = pltpu.roll(meta_own[...], KMAX * g, 1)
     m_own = pltpu.make_async_copy(meta_own, m_ref.at[0, g], own_sem.at[2])
     m_own.start()
-
-    pl.semaphore_wait(barrier, 12)
-    pl.semaphore_signal(ready.at[0], inc=1, device_id=below, device_id_type=MESH)
-
-    def occ_copy(src, d, dev):
-        return rcopy(occ_all.at[src], occ_all.at[src], occ_ss.at[d], occ_rs.at[src], dev)
-
-    def meta_copy(src, d, dev):
-        return rcopy(meta_own, m_ref.at[0, src], meta_ss.at[d], meta_rs.at[src], dev)
-
-    for d, p in enumerate(peers):
-        occ_copy(g, d, (p, a)).start()
-
-    def vy_copy(src, b, j):
-        return rcopy(
-            vir_ref.at[z, :, pl.ds(pl.multiple_of(xb[j] * 256, 256), 256)], v_ref[j].at[src, z],
-            vy_ss.at[b, j], vy_rs.at[b, j], (block[(1, 0, 2)[b]], a),
-        )
-
-    def half(ref, e):
-        return ref.at[64 * e:64 * e + 64, :]
-
-    for j in range(2):
-        for b in range(3):
-            vy_copy(g, b, j).start()
     for d, p in enumerate(peers):
         meta_copy(g, d, (p, a)).start()
 
@@ -248,15 +248,17 @@
         return pltpu.make_async_copy(tab_v.at[side], tab.at[side], tab_sem.at[side])
 
     def contract(side, j):
-        def group(p, carry):
-            for k in range(KMAX):
-                t = p * KMAX + k
+        def group(step, carry):
+            for n in range(2 * KMAX):
+                k = n % KMAX
+                p = 2 * step + n // KMAX
+                t = 2 * KMAX * step + n
                 piece = h_ref[side, k // CT, p, k % CT]
                 term = jnp.dot(piece, v_ref[j][p, tab[side, 1, t]], preferred_element_type=jnp.float32)
                 run[t + 1] = term + run[tab[side, 0, t]]
             return carry
 
-        lax.fori_loop(0, G, group, 0)
+        lax.fori_loop(0, G // 2, group, 0)
         for q in range(4):
             blocks = [run[tab[side, 2, 4 * q + b]] for b in range(4)]
             done[side, j, :, q * BLK:(q + 1) * BLK] = (
@@ -400,6 +402,42 @@
     )(rows, tiles, cols, aux, count, occ, vir)
 
 
+def widen_kernel(src, dst, narrow, wide, in_sem, out_sem):
+    pieces = 8
+    width = 16 * PDEV // pieces
+
+    def columns(ref, n):
+        return ref.at[:, n * width:(n + 1) * width]
+
+    loads = [pltpu.make_async_copy(columns(src, n), narrow.at[n], in_sem.at[n]) for n in range(pieces)]
+    stores = [pltpu.make_async_copy(wide.at[n], columns(dst, n), out_sem.at[n]) for n in range(pieces)]
+    for cp in loads:
+        cp.start()
+    for n in range(pieces):
+        loads[n].wait()
+        wide[n] = narrow[n].astype(jnp.float32)
+        stores[n].start()
+    for cp in stores:
+        cp.wait()
+
+
+def widen(result):
+    anywhere = pl.BlockSpec(memory_space=pl.ANY)
+    return pl.pallas_call(
+        widen_kernel,
+        out_shape=jax.ShapeDtypeStruct((64, 16 * PDEV), jnp.float32),
+        in_specs=[anywhere],
+        out_specs=anywhere,
+        scratch_shapes=[
+            pltpu.VMEM((8, 64, 2 * PDEV), jnp.bfloat16),
+            pltpu.VMEM((8, 64, 2 * PDEV), jnp.float32),
+            pltpu.SemaphoreType.DMA((8,)),
+            pltpu.SemaphoreType.DMA((8,)),
+        ],
+        name="widen",
+    )(result)
+
+
 def shards(integral_tiles, row_blocks, col_blocks, aux_blocks, tile_counts, occ_coeffs, vir_coeffs):
     result = whole(
         row_blocks.reshape(1, KMAX),
@@ -410,7 +448,7 @@
         occ_coeffs,
         vir_coeffs.reshape(4, BLK, V),
     )
-    return result.astype(jnp.float32)
+    return widen(result)
 
 
 def solution(mesh):

time: 51.7 us -> 51.2 us (level)
  other arithmetic: 2.68 us -> 0 us
  Pallas kernels: 48.2 us -> 50.4 us
    convert_element_type x1 -> x0, other arithmetic: 2.68 us -> none  [shards(): return result.astype(jnp.float32)]
    pallas_call x0 -> x1, Pallas kernels: none -> 2.37 us  [widen(): pl.pallas_call(widen_kernel, out_shape=jax.ShapeDtypeStruct((64, 16 * PDE...]
where the time goes in v4:
time: 51.2 us; the launch traced here: 51 us
  Pallas kernels  50.4 us (98%)
  between operations  0.66 us (1%)
    pallas_call x1, Pallas kernels, whole(): pl.pallas_call(whole_kernel, out_shape=jax.ShapeDtypeStruct((64, 16 * PDE...  48 us
    pallas_call x1, Pallas kernels, widen(): pl.pallas_call(widen_kernel, out_shape=jax.ShapeDtypeStruct((64, 16 * PDE...  2.37 us

profile of v4, /device:TPU:0, one launch (start us, length us, event | category | flops | bytes accessed | tf_op | source)
XLA Modules:
  0.0 51.0 jit_solution(5491040708788713037)
XLA Ops:
  0.7 48.0 %whole.1.src = bf16[64,8192]{1,0:T(8,128)(2,1)} custom-call(s32[1,12]{1,0:T(1,128)} %bitcast.7, bf16[12,32,128,128]{3,2,1,0:T(8,128)(2,1)} %bitcast.5, s32[1,12]{1,0:T(1,128)} %bitcast.8, s32[1,12]{1,0:T(1,128)} %bitcast.9, s32[1,1]{1,0:T(1,128)S(6)} %copy.8.count_ref, bf16[8,512]{1,0:T(8,128)(2,1)} %occ_ref.1, bf16[4,128,1024]{2,1,0:T(8,128)(2,1)} %bitcast.6), custom_call_target="tpu_custom_call" | custom-call | tf_op jit(solution)/shard_map/whole/pallas_call | solution.py:365
  48.6 2.4 %widen.1 = f32[64,8192]{1,0:T(8,128)} custom-call(bf16[64,8192]{1,0:T(8,128)(2,1)} %whole.1.src), custom_call_target="tpu_custom_call" | custom-call | tf_op jit(solution)/shard_map/widen/pallas_call | solution.py:426

commit v5 on v4

--- a/solution.py
+++ b/solution.py
@@ -15,7 +15,7 @@
 KMAX = 12
 G = 8
 NZ = 4
-CH = 4
+CH = 3
 CT = KMAX // CH
 MESH = pl.DeviceIdType.MESH
 
@@ -227,7 +227,7 @@
             start_z(1, 1)
         if chunk == 2:
             start_z(2, 1)
-        if chunk == 3:
+        if chunk == 2:
             m_own.wait()
             for d, p in enumerate(peers):
                 meta_copy(p, d, (p, a)).wait_recv()
@@ -309,9 +309,8 @@
     finish_z(2, 0)
     pass_z(0, 1)
     pass_z(1, 1)
+    pass_z(2, 1)
     forward_h(2)
-    pass_z(2, 1)
-    forward_h(3)
     for cp in tables:
         cp.wait()
     twins(0)

time: 51.2 us -> 50.3 us (0.982)
  Pallas kernels: 50.4 us -> 49.5 us
    pallas_call x1, Pallas kernels: 48 us -> 47.1 us  [whole(): pl.pallas_call(whole_kernel, out_shape=jax.ShapeDtypeStruct((64, 16 * PDE...]
where the time goes in v5:
time: 50.3 us; the launch traced here: 50.1 us
  Pallas kernels  49.5 us (98%)
  between operations  0.66 us (1%)
    pallas_call x1, Pallas kernels, whole(): pl.pallas_call(whole_kernel, out_shape=jax.ShapeDtypeStruct((64, 16 * PDE...  47.1 us
    pallas_call x1, Pallas kernels, widen(): pl.pallas_call(widen_kernel, out_shape=jax.ShapeDtypeStruct((64, 16 * PDE...  2.37 us

profile of v5, /device:TPU:0, one launch (start us, length us, event | category | flops | bytes accessed | tf_op | source)
XLA Modules:
  0.0 50.1 jit_solution(14880966720410191508)
XLA Ops:
  0.7 47.1 %whole.1.src = bf16[64,8192]{1,0:T(8,128)(2,1)} custom-call(s32[1,12]{1,0:T(1,128)} %bitcast.7, bf16[12,32,128,128]{3,2,1,0:T(8,128)(2,1)} %bitcast.5, s32[1,12]{1,0:T(1,128)} %bitcast.8, s32[1,12]{1,0:T(1,128)} %bitcast.9, s32[1,1]{1,0:T(1,128)S(6)} %copy.8.count_ref, bf16[8,512]{1,0:T(8,128)(2,1)} %occ_ref.1, bf16[4,128,1024]{2,1,0:T(8,128)(2,1)} %bitcast.6), custom_call_target="tpu_custom_call" | custom-call | tf_op jit(solution)/shard_map/whole/pallas_call | solution.py:364
  47.8 2.4 %widen.1 = f32[64,8192]{1,0:T(8,128)} custom-call(bf16[64,8192]{1,0:T(8,128)(2,1)} %whole.1.src), custom_call_target="tpu_custom_call" | custom-call | tf_op jit(solution)/shard_map/widen/pallas_call | solution.py:425
